TPU v7x, 32 devices: a whole 2x2x4 slice. The times are simulated.
32 devices in a mesh: dp: 8 (over z, y), chan: 4 (over x, core).
Axes of the slice: x: 2, y: 2, z: 4, core: 2. Of those that a mesh axis runs over, the one named last changes fastest.
Arguments:
- inputs: bfloat16 [16, 16, 16, 512], P('dp', None, None, 'chan'), may hold values from -6 to 6
- affine: float32 [3, 2, 512], P(None, None, 'chan'), may hold values from 0.3 to 1.3
- image_sizes: int32 [16, 2], P('dp'), may hold values from 8 to 16
- labels: int32 [16, 16, 16, 7], P('dp'), may hold values from 0 to 20
- label_mask: int32 [16, 16, 16, 7], P('dp'), may hold values 0 or 1
- unit_slots: int32 [54], replicated, may hold values from 0 to 55, as said below
- conv_master: float32 [56, 256, 512], P('dp', None, 'chan'), may hold values from -0.09375 to 0.09375
- conv_first: float32 [56, 256, 512], P('dp', None, 'chan'), may hold values from -0.00390625 to 0.00390625
- conv_second: float32 [56, 256, 512], P('dp', None, 'chan'), may hold values from 2.746582e-09 to 4.3945313e-08
- head_master: float32 [7, 256, 512], P(None, 'chan'), may hold values from -0.25 to 0.25
- head_first: float32 [7, 256, 512], P(None, 'chan'), may hold values from -0.0048828125 to 0.0048828125
- head_second: float32 [7, 256, 512], P(None, 'chan'), may hold values from 4.8828124e-09 to 7.8125e-08
- join_master: float32 [7, 256, 21], P(None, 'chan'), may hold values from -4 to 4
- join_first: float32 [7, 256, 21], P(None, 'chan'), may hold values from -0.0012207031 to 0.0012207031
- join_second: float32 [7, 256, 21], P(None, 'chan'), may hold values from 3.0517577e-10 to 4.8828124e-09
- scale_master: float32 [7, 256], P(None, 'chan'), may hold values from 1 to 4
- scale_first: float32 [7, 256], P(None, 'chan'), may hold values from -0.0024414062 to 0.0024414062
- scale_second: float32 [7, 256], P(None, 'chan'), may hold values from 1.2207031e-09 to 1.953125e-08
- step_count: int32 [1], replicated, may hold values from 2 to 20
Outputs:
- loss: float32 [1], replicated
- conv_new: float32 [56, 256, 512], P('dp', None, 'chan')
- conv_first_new: float32 [56, 256, 512], P('dp', None, 'chan')
- conv_second_new: float32 [56, 256, 512], P('dp', None, 'chan')
- head_new: float32 [7, 256, 512], P(None, 'chan')
- head_first_new: float32 [7, 256, 512], P(None, 'chan')
- head_second_new: float32 [7, 256, 512], P(None, 'chan')
- join_new: float32 [7, 256, 21], P(None, 'chan')
- join_first_new: float32 [7, 256, 21], P(None, 'chan')
- join_second_new: float32 [7, 256, 21], P(None, 'chan')
- scale_new: float32 [7, 256], P(None, 'chan')
- scale_first_new: float32 [7, 256], P(None, 'chan')
- scale_second_new: float32 [7, 256], P(None, 'chan')
Inputs may be any that keep to these rules, and one draw needn't show every extreme that they name: `unit_slots`: distinct slots; slot s belongs to index s // 7 of dp, so an index holds at most 7 blocks; slot 55 is always used.
All inputs are finite; a program needn't handle non-finite values. No bound on the sum of `label_mask` on one device may be relied on, other than what follows from the above.
Results may differ from a plain program's by a relative error of at most 0.0035.
The roundings to bfloat16 on the way count: a program that leaves them out, or rounds other values in their place, can miss the bound.
Values may be sent and summed in bfloat16 or wider, within the bound.
A program may use at most 128 MiB of HBM per device.

v0:
```python
import jax
import jax.numpy as jnp
from jax import lax
from jax.sharding import PartitionSpec as P

C = 512
K = 21
TASKS = 7
LAYERS = 3
H = 16
W = 16
beta_one = 0.9
beta_two = 0.999
eps_adam = 1e-08
decay_rate = 0.01
eps_norm = 1e-06


def valid_pixels(image_sizes):
    row_ids = jnp.arange(H)[None, :, None] < image_sizes[:, 0][:, None, None]
    col_ids = jnp.arange(W)[None, None, :] < image_sizes[:, 1][:, None, None]
    return (row_ids & col_ids).astype(jnp.float32)[..., None]


def adamw(weight, gradient, moment_one, moment_two, step_rate, step_count):
    step_float = step_count[0].astype(jnp.float32)
    moment_one = beta_one * moment_one + (1.0 - beta_one) * gradient
    moment_two = beta_two * moment_two + (1.0 - beta_two) * gradient * gradient
    first_hat = moment_one / (1.0 - beta_one**step_float)
    second_hat = moment_two / (1.0 - beta_two**step_float)
    weight = weight - step_rate * (
        first_hat / (jnp.sqrt(second_hat) + eps_adam) + decay_rate * weight
    )
    return (weight, moment_one, moment_two)


def pad_image(values):
    return jnp.pad(values, ((0, 0), (1, 1), (1, 1), (0, 0)))


def gather_channels(local_part):
    return lax.all_gather(local_part, "chan", axis=3, tiled=True)


def channel_sum(partial_term):
    return lax.psum_scatter(partial_term, "chan", scatter_dimension=3, tiled=True)


def conv_forward(gathered, kernels):
    padded = pad_image(gathered)
    summed = jnp.zeros(gathered.shape[:3] + (kernels.shape[2],), jnp.float32)
    for tap_index in range(9):
        row_shift, col_shift = divmod(tap_index, 3)
        window = padded[:, row_shift : row_shift + H, col_shift : col_shift + W, :]
        summed = summed + jnp.einsum(
            "ihwc,cd->ihwd", window, kernels[tap_index], preferred_element_type=jnp.float32
        )
    return summed


def conv_backward(gathered, grad_linear, kernels, need_input):
    padded = pad_image(gathered)
    grad_padded = pad_image(grad_linear)
    weight_grads = []
    spread_sum = jnp.zeros(gathered.shape, jnp.float32)
    for tap_index in range(9):
        row_shift, col_shift = divmod(tap_index, 3)
        window = padded[:, row_shift : row_shift + H, col_shift : col_shift + W, :]
        weight_grads.append(
            jnp.einsum("ihwc,ihwd->cd", window, grad_linear, preferred_element_type=jnp.float32)
        )
        if need_input:
            back_window = grad_padded[
                :, 2 - row_shift : 2 - row_shift + H, 2 - col_shift : 2 - col_shift + W, :
            ]
            spread_sum = spread_sum + jnp.einsum(
                "ihwd,cd->ihwc", back_window, kernels[tap_index], preferred_element_type=jnp.float32
            )
    input_grad = channel_sum(spread_sum) if need_input else None
    return (jnp.stack(weight_grads), input_grad)


def per_device(
    inputs,
    affine,
    image_sizes,
    labels,
    label_mask,
    unit_slots,
    conv_master,
    conv_first,
    conv_second,
    head_master,
    head_first,
    head_second,
    join_master,
    join_first,
    join_second,
    scale_master,
    scale_first,
    scale_second,
    step_count,
):
    inside = valid_pixels(image_sizes)
    slot_count = conv_master.shape[0]
    every_slot = lax.all_gather(conv_master.astype(jnp.bfloat16), "dp", axis=0, tiled=True)
    blocks = jnp.take(every_slot, unit_slots, axis=0)
    kernels = blocks.reshape(LAYERS, 9, C, blocks.shape[2])
    head_low = head_master.astype(jnp.bfloat16)
    join_low = join_master.astype(jnp.bfloat16)
    label_keep = label_mask.astype(jnp.float32) * inside
    counts = jnp.maximum(lax.psum(jnp.sum(label_keep, axis=(0, 1, 2)), "dp"), 1.0)
    current = (inputs.astype(jnp.float32) * inside).astype(jnp.bfloat16)
    gathered_list, linear_list, local_list = ([], [], [])
    for layer_index in range(LAYERS):
        gathered = gather_channels(current)
        linear = conv_forward(gathered, kernels[layer_index])
        output = (jax.nn.relu(linear) * affine[layer_index, 0] + affine[layer_index, 1]) * inside
        gathered_list.append(gathered)
        linear_list.append(linear)
        local_list.append(current)
        current = output.astype(jnp.bfloat16)
    features = gather_channels(current)
    flat_features = features.reshape(-1, C)
    hidden = jnp.einsum("pc,tdc->ptd", flat_features, head_low, preferred_element_type=jnp.float32)
    squares = lax.psum(jnp.sum(hidden * hidden, axis=2), "chan")
    inverse = lax.rsqrt(squares + eps_norm)[:, :, None]
    normed = hidden * inverse
    scaled = (scale_master[None] * normed).astype(jnp.bfloat16)
    partial_logits = jnp.einsum(
        "ptd,tdk->ptk", scaled, join_low, preferred_element_type=jnp.float32
    )
    logits = lax.psum(partial_logits, "chan")
    largest = jnp.max(logits, axis=2, keepdims=True)
    shifted = jnp.exp(logits - largest)
    totals = jnp.sum(shifted, axis=2, keepdims=True)
    log_norm = largest[..., 0] + jnp.log(totals[..., 0])
    onehot = (labels.reshape(-1, TASKS)[:, :, None] == jnp.arange(K)[None, None, :]).astype(
        jnp.float32
    )
    picked = jnp.sum(onehot * logits, axis=2)
    pixel_weight = label_keep.reshape(-1, TASKS) / counts[None, :]
    loss_local = jnp.sum(pixel_weight * (log_norm - picked))
    grad_logits = (pixel_weight[:, :, None] * (shifted / totals - onehot)).astype(jnp.bfloat16)
    grad_scaled = jnp.einsum(
        "ptk,tdk->ptd", grad_logits, join_low, preferred_element_type=jnp.float32
    )
    join_grad = jnp.einsum("ptd,ptk->tdk", scaled, grad_logits, preferred_element_type=jnp.float32)
    scale_grad = jnp.sum(grad_scaled * normed, axis=0)
    grad_normed = grad_scaled * scale_master[None]
    along_norm = lax.psum(jnp.sum(normed * grad_normed, axis=2), "chan")[:, :, None]
    grad_hidden = ((grad_normed - normed * along_norm) * inverse).astype(jnp.bfloat16)
    head_grad = jnp.einsum(
        "ptd,pc->tdc", grad_hidden, flat_features, preferred_element_type=jnp.float32
    )
    grad_flat = jnp.einsum("ptd,tdc->pc", grad_hidden, head_low, preferred_element_type=jnp.float32)
    grad_current = channel_sum(grad_flat.reshape(features.shape))
    conv_grads = [None] * LAYERS
    for layer_index in reversed(range(LAYERS)):
        linear = linear_list[layer_index]
        scaled_back = grad_current * inside * affine[layer_index, 0]
        grad_linear = jnp.where(linear > 0, scaled_back, 0.0).astype(jnp.bfloat16)
        gathered = gathered_list[layer_index]
        conv_grads[layer_index], grad_current = conv_backward(
            gathered, grad_linear, kernels[layer_index], layer_index > 0
        )
    unit_grads = jnp.stack(conv_grads).reshape(-1, C // 2, kernels.shape[3])
    summed_all = lax.psum(unit_grads, "dp")
    slot_base = lax.axis_index("dp") * slot_count
    picking = ((slot_base + jnp.arange(slot_count))[:, None] == unit_slots[None, :]).astype(
        jnp.float32
    )
    slot_grads = jnp.einsum("su,urc->src", picking, summed_all, precision=lax.Precision.HIGHEST)
    head_total, join_total, scale_total, loss_total = lax.psum(
        (head_grad, join_grad, scale_grad, loss_local), "dp"
    )
    conv_out = adamw(conv_master, slot_grads, conv_first, conv_second, 0.01, step_count)
    head_out = adamw(head_master, head_total, head_first, head_second, 0.03, step_count)
    join_out = adamw(join_master, join_total, join_first, join_second, 0.4, step_count)
    scale_out = adamw(scale_master, scale_total, scale_first, scale_second, 0.8, step_count)
    return (loss_total.reshape(1),) + conv_out + head_out + join_out + scale_out


def solution(mesh):
    placed = (
        P("dp", None, None, "chan"),
        P(None, None, "chan"),
        P("dp", None),
        P("dp", None, None, None),
        P("dp", None, None, None),
        P(),
        P("dp", None, "chan"),
        P("dp", None, "chan"),
        P("dp", None, "chan"),
        P(None, "chan", None),
        P(None, "chan", None),
        P(None, "chan", None),
        P(None, "chan", None),
        P(None, "chan", None),
        P(None, "chan", None),
        P(None, "chan"),
        P(None, "chan"),
        P(None, "chan"),
        P(),
    )
    return jax.shard_map(
        per_device,
        mesh=mesh,
        in_specs=placed,
        out_specs=(
            P(),
            P("dp", None, "chan"),
            P("dp", None, "chan"),
            P("dp", None, "chan"),
            P(None, "chan", None),
            P(None, "chan", None),
            P(None, "chan", None),
            P(None, "chan", None),
            P(None, "chan", None),
            P(None, "chan", None),
            P(None, "chan"),
            P(None, "chan"),
            P(None, "chan"),
        ),
        check_vma=False,
    )
```

profile of v0, /device:TPU:0, one launch (start us, length us, event | category | flops | bytes accessed | tf_op | source)
XLA Modules:
  0.0 576.6 jit_solution(2468389914004056909)
XLA Ops:
  7.3 2.0 convert_element_type.77
  9.4 1.0 slice_reduce_fusion.1
  10.5 1.1 fusion.130
  11.5 23.7 %psum.63 = f32[7]{0:T(128)S(1)} all-reduce(f32[7]{0:T(128)S(1)} %get-tuple-element.75), channel_id=1, replica_groups=mesh['dp'=8,'chan'=4] {'dp'}, use_global_device_ids=true, to_apply=%region_1.2 | all-reduce | flops 7 | bytes 56 | tf_op jit(solution)/shard_map/psum | solution.py:112
  36.5 7.2 %all_gather.15 = bf16[2,16,16,512]{3,2,1,0:T(8,128)(2,1)S(1)} all-gather(bf16[2,16,16,128]{3,2,1,0:T(8,128)(2,1)S(1)} %multiply_convert_fusion.6), channel_id=1, replica_groups=mesh['dp'=8,'chan'=4] {'chan'}, dimensions={3}, use_global_device_ids=true | all-gather | bytes 655360 | tf_op jit(solution)/shard_map/all_gather | solution.py:42
  43.8 36.1 %all-gather.2.cloned.1.call-done = bf16[56,256,128]{2,1,0:T(8,128)(2,1)} async-done(((bf16[7,256,128]{2,1,0:T(8,128)(2,1)}), bf16[56,256,128]{2,1,0:T(8,128)(2,1)}) %all-gather.2.cloned.1.call-update) | async-done | bytes 3670032 | tf_op jit(solution)/shard_map/all_gather | solution.py:106
  79.9 4.9 gather_fusion
  84.8 2.4 broadcast_select_fusion
  90.1 1.0 multiply_convert_fusion.5
  91.1 7.2 %all_gather.17 = bf16[2,16,16,512]{3,2,1,0:T(8,128)(2,1)S(1)} all-gather(bf16[2,16,16,128]{3,2,1,0:T(8,128)(2,1)S(1)} %get-tuple-element.134), channel_id=1, replica_groups=mesh['dp'=8,'chan'=4] {'chan'}, dimensions={3}, use_global_device_ids=true | all-gather | bytes 655360 | tf_op jit(solution)/shard_map/all_gather | solution.py:42
  100.9 1.0 multiply_convert_fusion.4
  101.9 7.3 %all_gather.18 = bf16[2,16,16,512]{3,2,1,0:T(8,128)(2,1)S(1)} all-gather(bf16[2,16,16,128]{3,2,1,0:T(8,128)(2,1)S(1)} %get-tuple-element.136), channel_id=1, replica_groups=mesh['dp'=8,'chan'=4] {'chan'}, dimensions={3}, use_global_device_ids=true | all-gather | bytes 655360 | tf_op jit(solution)/shard_map/all_gather | solution.py:42
  111.8 1.0 multiply_convert_fusion.3
  112.8 7.3 %all_gather.19 = bf16[2,16,16,512]{3,2,1,0:T(8,128)(2,1)S(1)} all-gather(bf16[2,16,16,128]{3,2,1,0:T(8,128)(2,1)S(1)} %get-tuple-element.138), channel_id=1, replica_groups=mesh['dp'=8,'chan'=4] {'chan'}, dimensions={3}, use_global_device_ids=true | all-gather | bytes 655360 | tf_op jit(solution)/shard_map/all_gather | solution.py:42
  120.5 10.7 %psum.64 = f32[512,7]{0,1:T(8,128)S(1)} all-reduce(f32[512,7]{0,1:T(8,128)S(1)} %get-tuple-element.140), channel_id=1, replica_groups=mesh['dp'=8,'chan'=4] {'chan'}, use_global_device_ids=true, to_apply=%region_3.4 | all-reduce | flops 3584 | bytes 28672 | tf_op jit(solution)/shard_map/psum | solution.py:126
  131.3 1.0 convolution_bitcast_fusion.1
  132.5 30.9 %all-reduce.10.cloned.1.call-done = f32[512,7,21]{0,2,1:T(8,128)} async-done(((f32[512,7,21]{0,2,1:T(8,128)}), f32[512,7,21]{0,2,1:T(8,128)}) %all-reduce.10.cloned.1.call-update) | async-done | bytes 301072 | tf_op jit(solution)/shard_map/psum | solution.py:133
  163.4 1.0 reduce_max.9
  164.4 1.7 fusion.59
  166.2 2.8 multiply_reduce_fusion
  169.0 10.6 %psum.67 = f32[512,7]{0,1:T(8,128)S(1)} all-reduce(f32[512,7]{0,1:T(8,128)S(1)} %get-tuple-element.53), channel_id=1, replica_groups=mesh['dp'=8,'chan'=4] {'chan'}, use_global_device_ids=true, to_apply=%region_11.12 | all-reduce | flops 3584 | bytes 28672 | tf_op jit(solution)/shard_map/psum | solution.py:151
  179.6 1.4 multiply_convert_fusion
  181.0 2.7 fusion.60
  183.8 2.3 pad_slice_fusion.16
  186.2 2.3 pad_slice_fusion
  188.5 2.3 pad_slice_fusion.8
  190.9 1.3 fusion.134
  192.2 16.6 %reduce-scatter.4.cloned.1.call-done = f32[2,16,16,128]{3,2,1,0:T(8,128)} async-done(((f32[2,16,16,512]{3,2,1,0:T(8,128)}), f32[2,16,16,128]{3,2,1,0:T(8,128)}) %reduce-scatter.4.cloned.1.call-update) | async-done | bytes 262160 | tf_op jit(solution)/shard_map/reduce_scatter | solution.py:46
  208.8 1.1 select_convert_fusion.2
  209.9 1.2 fusion.66
  211.1 1.2 convolution_add_fusion.15
  215.1 1.3 convolution_add_fusion.8
  216.5 2.1 fusion.8
  218.6 1.0 fusion.7
  219.6 1.0 fusion.6
  220.7 1.0 fusion.5
  221.7 1.0 fusion.4
  222.8 1.1 fusion.3
  223.8 1.0 fusion.2
  224.9 1.1 fusion.1
  226.0 1.0 fusion
  227.0 14.3 %reduce-scatter.6.cloned.1.call-done = f32[2,16,16,128]{3,2,1,0:T(8,128)} async-done(((f32[2,16,16,512]{3,2,1,0:T(8,128)}), f32[2,16,16,128]{3,2,1,0:T(8,128)}) %reduce-scatter.6.cloned.1.call-update) | async-done | bytes 262160 | tf_op jit(solution)/shard_map/reduce_scatter | solution.py:46
  241.3 1.1 select_convert_fusion.1
  245.8 1.3 convolution_add_fusion
  247.4 1.0 fusion.17
  248.4 1.0 fusion.16
  249.5 1.0 fusion.15
  250.5 1.0 fusion.14
  251.5 1.0 fusion.13
  252.6 1.1 fusion.12
  253.7 1.0 fusion.11
  254.8 1.0 fusion.10
  255.8 1.0 fusion.9
  256.9 15.2 %reduce-scatter.8.cloned.1.call-done = f32[2,16,16,128]{3,2,1,0:T(8,128)} async-done(((f32[2,16,16,512]{3,2,1,0:T(8,128)}), f32[2,16,16,128]{3,2,1,0:T(8,128)}) %reduce-scatter.8.cloned.1.call-update) | async-done | bytes 262160 | tf_op jit(solution)/shard_map/reduce_scatter | solution.py:46
  272.1 1.1 select_convert_fusion
  278.5 2.9 pad_maximum_fusion
  281.4 7.1 %copy.215 = f32[54,256,128]{2,0,1:T(8,128)} copy(f32[54,256,128]{2,1,0:T(8,128)S(1)} %bitcast.450) | data formatting | bytes 14155776 | tf_op jit(solution)/shard_map/reshape | solution.py:167
  290.9 41.8 %all-reduce.5 = (f32[1]{0:T(128)}, f32[7,64,21]{1,2,0:T(8,128)S(1)}, f32[7,64]{1,0:T(8,128)S(1)}) all-reduce(f32[1]{0:T(128)} %bitcast.90, f32[7,64,21]{1,2,0:T(8,128)S(1)} %fusion.69, f32[7,64]{1,0:T(8,128)S(1)} %copy-done.86), channel_id=1, replica_groups=mesh['dp'=8,'chan'=4] {'dp'}, use_global_device_ids=true, to_apply=%region_9.10 | all-reduce | flops 9857 | bytes 78856 | tf_op jit(solution)/shard_map/psum | solution.py:174
  334.1 221.9 %all-reduce.12.cloned.1.call-done = (f32[54,256,128]{2,0,1:T(8,128)}, f32[7,64,512]{2,1,0:T(8,128)}) async-done(((f32[54,256,128]{2,0,1:T(8,128)}, f32[7,64,512]{2,1,0:T(8,128)}), (f32[54,256,128]{2,0,1:T(8,128)}, f32[7,64,512]{2,1,0:T(8,128)})) %all-reduce.12.cloned.1.call-update) | async-done | bytes 7995408 | tf_op jit(solution)/shard_map/psum | solution.py:168
  556.0 7.8 %copy_subtract_fusion = (f32[7,256,128]{2,0,1:T(8,128)S(1)}, f32[7,256,128]{2,0,1:T(8,128)S(1)}, f32[7,256,128]{2,0,1:T(8,128)S(1)}) fusion(f32[7,256,128]{2,1,0:T(8,128)S(1)} %copy-done, f32[]{:T(128)} %bitcast.217, f32[]{:T(128)} %bitcast.216, f32[7,256,128]{2,1,0:T(8,128)} %param.27, f32[7,256,128]{2,1,0:T(8,128)} %param.26, ...), kind=kOutput, calls=%fused_computation.126 | convolution fusion | flops 152076672 | bytes 12583164 | tf_op jit(solution)/shard_map/su,urc->src/dot_general | solution.py:173
  563.7 1.1 copy.219
  564.8 1.1 copy.220
  565.9 1.1 copy.221
  567.5 2.0 multiply_subtract_fusion
  (272 shorter events, 24.7 us)
Async XLA Ops:
  7.2 29.1 %copy-start.92 = (s32[54]{0:T(128)S(1)}, s32[54]{0:T(128)}, u32[]{:S(2)}) copy-start(s32[54]{0:T(128)} %param.24) | copy-start | bytes 652
  7.2 29.2 %copy-start.71 = (bf16[2,16,16,128]{3,2,1,0:T(8,128)(2,1)S(1)}, bf16[2,16,16,128]{3,2,1,0:T(8,128)(2,1)}, u32[]{:S(2)}) copy-start(bf16[2,16,16,128]{3,2,1,0:T(8,128)(2,1)} %param.19) | copy-start | bytes 393220
  7.2 36.5 %copy-start.89 = (f32[3,2,128]{2,1,0:T(2,128)S(1)}, f32[3,2,128]{2,1,0:T(2,128)}, u32[]{:S(2)}) copy-start(f32[3,2,128]{2,1,0:T(2,128)} %param.20) | copy-start | bytes 9220
  7.2 72.7 %all-gather.2.cloned.1.call-start = ((), (), s32[]{:S(2)}) async-start(), calls=%async_computation.3 | async-start | bytes 4128768 | tf_op jit(solution)/shard_map/all_gather | solution.py:106
  9.3 154.1 %all-reduce.10.cloned.1.call-start = ((), (), s32[]{:S(2)}) async-start(), calls=%async_computation.4 | async-start | bytes 688128 | tf_op jit(solution)/shard_map/psum | solution.py:133
  11.5 73.2 %copy-start.41 = (f32[2,16,16,7]{2,1,0,3:T(8,128)}, f32[2,16,16,7]{2,1,0,3:T(8,128)S(1)}, u32[]{:S(2)}) copy-start(f32[2,16,16,7]{2,1,0,3:T(8,128)S(1)} %get-tuple-element.76) | copy-start | bytes 43012
  36.2 130.0 %copy-start.75 = (s32[512,7]{0,1:T(8,128)}, s32[512,7]{0,1:T(8,128)S(1)}, u32[]{:S(2)}) copy-start(s32[512,7]{0,1:T(8,128)S(1)} %eq.28) | copy-start | bytes 43012
  43.7 88.6 %copy-start.90 = (f32[7]{0:T(128)}, f32[7]{0:T(128)S(1)}, u32[]{:S(2)}) copy-start(f32[7]{0:T(128)S(1)} %broadcast_maximum_fusion) | copy-start | bytes 88
  43.8 46.3 %copy-start.81 = (f32[128]{0:T(128)}, f32[128]{0:T(128)S(1)}, u32[]{:S(2)}) copy-start(f32[128]{0:T(128)S(1)} %get-tuple-element.132) | copy-start | bytes 1540
  43.8 57.1 %copy-start.83 = (f32[128]{0:T(128)}, f32[128]{0:T(128)S(1)}, u32[]{:S(2)}) copy-start(f32[128]{0:T(128)S(1)} %get-tuple-element.130) | copy-start | bytes 1540
  43.8 68.0 %copy-start.85 = (f32[128]{0:T(128)}, f32[128]{0:T(128)S(1)}, u32[]{:S(2)}) copy-start(f32[128]{0:T(128)S(1)} %get-tuple-element.128) | copy-start | bytes 1540
  87.3 11.0 %copy-start.20 = (bf16[2,256,128]{2,1,0:T(8,128)(2,1)}, bf16[2,256,128]{2,1,0:T(8,128)(2,1)S(1)}, u32[]{:S(2)}) copy-start(bf16[2,256,128]{2,1,0:T(8,128)(2,1)S(1)} %get-tuple-element.94) | copy-start | bytes 393220
  87.3 11.3 %copy-start.18 = (bf16[2,256,128]{2,1,0:T(8,128)(2,1)}, bf16[2,256,128]{2,1,0:T(8,128)(2,1)S(1)}, u32[]{:S(2)}) copy-start(bf16[2,256,128]{2,1,0:T(8,128)(2,1)S(1)} %get-tuple-element.93) | copy-start | bytes 393220
  87.4 11.6 %copy-start.16 = (bf16[2,256,128]{2,1,0:T(8,128)(2,1)}, bf16[2,256,128]{2,1,0:T(8,128)(2,1)S(1)}, u32[]{:S(2)}) copy-start(bf16[2,256,128]{2,1,0:T(8,128)(2,1)S(1)} %get-tuple-element.92) | copy-start | bytes 393220
  87.4 11.9 %copy-start.14 = (bf16[2,256,128]{2,1,0:T(8,128)(2,1)}, bf16[2,256,128]{2,1,0:T(8,128)(2,1)S(1)}, u32[]{:S(2)}) copy-start(bf16[2,256,128]{2,1,0:T(8,128)(2,1)S(1)} %get-tuple-element.91) | copy-start | bytes 393220
  87.4 12.2 %copy-start.12 = (bf16[2,256,128]{2,1,0:T(8,128)(2,1)}, bf16[2,256,128]{2,1,0:T(8,128)(2,1)S(1)}, u32[]{:S(2)}) copy-start(bf16[2,256,128]{2,1,0:T(8,128)(2,1)S(1)} %get-tuple-element.90) | copy-start | bytes 393220
  87.4 12.5 %copy-start.10 = (bf16[2,256,128]{2,1,0:T(8,128)(2,1)}, bf16[2,256,128]{2,1,0:T(8,128)(2,1)S(1)}, u32[]{:S(2)}) copy-start(bf16[2,256,128]{2,1,0:T(8,128)(2,1)S(1)} %get-tuple-element.89) | copy-start | bytes 393220
  87.4 12.8 %copy-start.8 = (bf16[2,256,128]{2,1,0:T(8,128)(2,1)}, bf16[2,256,128]{2,1,0:T(8,128)(2,1)S(1)}, u32[]{:S(2)}) copy-start(bf16[2,256,128]{2,1,0:T(8,128)(2,1)S(1)} %get-tuple-element.88) | copy-start | bytes 393220
  87.4 13.1 %copy-start.6 = (bf16[2,256,128]{2,1,0:T(8,128)(2,1)}, bf16[2,256,128]{2,1,0:T(8,128)(2,1)S(1)}, u32[]{:S(2)}) copy-start(bf16[2,256,128]{2,1,0:T(8,128)(2,1)S(1)} %get-tuple-element.87) | copy-start | bytes 393220
  87.4 13.4 %copy-start.4 = (bf16[2,256,128]{2,1,0:T(8,128)(2,1)}, bf16[2,256,128]{2,1,0:T(8,128)(2,1)S(1)}, u32[]{:S(2)}) copy-start(bf16[2,256,128]{2,1,0:T(8,128)(2,1)S(1)} %get-tuple-element.86) | copy-start | bytes 393220
  87.4 21.7 %copy-start.37 = (bf16[2,256,128]{2,1,0:T(8,128)(2,1)}, bf16[2,256,128]{2,1,0:T(8,128)(2,1)S(1)}, u32[]{:S(2)}) copy-start(bf16[2,256,128]{2,1,0:T(8,128)(2,1)S(1)} %get-tuple-element.85) | copy-start | bytes 393220
  87.4 22.1 %copy-start.36 = (bf16[2,256,128]{2,1,0:T(8,128)(2,1)}, bf16[2,256,128]{2,1,0:T(8,128)(2,1)S(1)}, u32[]{:S(2)}) copy-start(bf16[2,256,128]{2,1,0:T(8,128)(2,1)S(1)} %get-tuple-element.84) | copy-start | bytes 393220
  87.4 22.4 %copy-start.34 = (bf16[2,256,128]{2,1,0:T(8,128)(2,1)}, bf16[2,256,128]{2,1,0:T(8,128)(2,1)S(1)}, u32[]{:S(2)}) copy-start(bf16[2,256,128]{2,1,0:T(8,128)(2,1)S(1)} %get-tuple-element.83) | copy-start | bytes 393220
  87.5 22.7 %copy-start.32 = (bf16[2,256,128]{2,1,0:T(8,128)(2,1)}, bf16[2,256,128]{2,1,0:T(8,128)(2,1)S(1)}, u32[]{:S(2)}) copy-start(bf16[2,256,128]{2,1,0:T(8,128)(2,1)S(1)} %get-tuple-element.82) | copy-start | bytes 393220
  87.5 23.0 %copy-start.30 = (bf16[2,256,128]{2,1,0:T(8,128)(2,1)}, bf16[2,256,128]{2,1,0:T(8,128)(2,1)S(1)}, u32[]{:S(2)}) copy-start(bf16[2,256,128]{2,1,0:T(8,128)(2,1)S(1)} %get-tuple-element.81) | copy-start | bytes 393220
  87.5 23.3 %copy-start.28 = (bf16[2,256,128]{2,1,0:T(8,128)(2,1)}, bf16[2,256,128]{2,1,0:T(8,128)(2,1)S(1)}, u32[]{:S(2)}) copy-start(bf16[2,256,128]{2,1,0:T(8,128)(2,1)S(1)} %get-tuple-element.80) | copy-start | bytes 393220
  87.5 23.6 %copy-start.26 = (bf16[2,256,128]{2,1,0:T(8,128)(2,1)}, bf16[2,256,128]{2,1,0:T(8,128)(2,1)S(1)}, u32[]{:S(2)}) copy-start(bf16[2,256,128]{2,1,0:T(8,128)(2,1)S(1)} %get-tuple-element.79) | copy-start | bytes 393220
  87.5 23.9 %copy-start.24 = (bf16[2,256,128]{2,1,0:T(8,128)(2,1)}, bf16[2,256,128]{2,1,0:T(8,128)(2,1)S(1)}, u32[]{:S(2)}) copy-start(bf16[2,256,128]{2,1,0:T(8,128)(2,1)S(1)} %get-tuple-element.78) | copy-start | bytes 393220
  87.5 24.3 %copy-start.22 = (bf16[2,256,128]{2,1,0:T(8,128)(2,1)}, bf16[2,256,128]{2,1,0:T(8,128)(2,1)S(1)}, u32[]{:S(2)}) copy-start(bf16[2,256,128]{2,1,0:T(8,128)(2,1)S(1)} %get-tuple-element.77) | copy-start | bytes 393220
  111.1 9.0 %copy-start.1 = (f32[7,64,512]{2,1,0:T(8,128)S(1)}, f32[7,64,512]{2,1,0:T(8,128)}, u32[]{:S(2)}) copy-start(f32[7,64,512]{2,1,0:T(8,128)} %param.28) | copy-start | bytes 2752516
  111.7 19.5 %copy-start.69 = (f32[7,64,21]{1,2,0:T(8,128)S(1)}, f32[7,64,21]{1,2,0:T(8,128)}, u32[]{:S(2)}) copy-start(f32[7,64,21]{1,2,0:T(8,128)} %param.31) | copy-start | bytes 112900
  111.8 19.5 %copy-start.77 = (f32[7,64]{1,0:T(8,128)S(1)}, f32[7,64]{1,0:T(8,128)}, u32[]{:S(2)}) copy-start(f32[7,64]{1,0:T(8,128)} %param.34) | copy-start | bytes 5380
  132.3 76.5 %reduce-scatter.4.cloned.1.call-start = ((), (), s32[]{:S(2)}) async-start(), calls=%async_computation.5 | async-start | bytes 1310720 | tf_op jit(solution)/shard_map/reduce_scatter | solution.py:46
  132.5 47.1 %copy-start.79 = (f32[512,7]{0,1:T(8,128)}, f32[512,7]{0,1:T(8,128)S(1)}, u32[]{:S(2)}) copy-start(f32[512,7]{0,1:T(8,128)S(1)} %broadcast_divide_fusion) | copy-start | bytes 43012
  183.7 57.6 %reduce-scatter.6.cloned.1.call-start = ((), (), s32[]{:S(2)}) async-start(), calls=%async_computation.6 | async-start | bytes 1310720 | tf_op jit(solution)/shard_map/reduce_scatter | solution.py:46
  183.8 2.4 copy-start.40
  183.8 2.4 copy-start.39
  192.2 20.2 %copy-start.35 = (bf16[2,256,128]{2,1,0:T(8,128)(2,1)S(1)}, bf16[2,256,128]{2,1,0:T(8,128)(2,1)}, u32[]{:S(2)}) copy-start(bf16[2,256,128]{2,1,0:T(8,128)(2,1)} %copy-done.34) | copy-start | bytes 393220
  216.4 2.2 copy-start.68
  216.4 55.6 %reduce-scatter.8.cloned.1.call-start = ((), (), s32[]{:S(2)}) async-start(), calls=%async_computation.7 | async-start | bytes 1310720 | tf_op jit(solution)/shard_map/reduce_scatter | solution.py:46
  225.9 15.4 %copy-start.84 = (f32[128]{0:T(128)S(1)}, f32[128]{0:T(128)}, u32[]{:S(2)}) copy-start(f32[128]{0:T(128)} %copy-done.83) | copy-start | bytes 1540
  225.9 16.5 %copy-start.21 = (bf16[2,256,128]{2,1,0:T(8,128)(2,1)S(1)}, bf16[2,256,128]{2,1,0:T(8,128)(2,1)}, u32[]{:S(2)}) copy-start(bf16[2,256,128]{2,1,0:T(8,128)(2,1)} %copy-done.20) | copy-start | bytes 393220
  225.9 16.8 %copy-start.19 = (bf16[2,256,128]{2,1,0:T(8,128)(2,1)S(1)}, bf16[2,256,128]{2,1,0:T(8,128)(2,1)}, u32[]{:S(2)}) copy-start(bf16[2,256,128]{2,1,0:T(8,128)(2,1)} %copy-done.18) | copy-start | bytes 393220
  227.0 16.1 %copy-start.17 = (bf16[2,256,128]{2,1,0:T(8,128)(2,1)S(1)}, bf16[2,256,128]{2,1,0:T(8,128)(2,1)}, u32[]{:S(2)}) copy-start(bf16[2,256,128]{2,1,0:T(8,128)(2,1)} %copy-done.16) | copy-start | bytes 393220
  247.2 308.8 %all-reduce.12.cloned.1.call-start = ((), (), s32[]{:S(2)}) async-start(), calls=%async_computation.8 | async-start | bytes 16515072 | tf_op jit(solution)/shard_map/psum | solution.py:168
  255.8 16.3 %copy-start.38 = (f32[2,16,16,128]{3,2,1,0:T(8,128)S(1)}, f32[2,16,16,128]{3,2,1,0:T(8,128)}, u32[]{:S(2)}) copy-start(f32[2,16,16,128]{3,2,1,0:T(8,128)} %get-tuple-element.135) | copy-start | bytes 786436
  255.8 16.3 %copy-start.82 = (f32[128]{0:T(128)S(1)}, f32[128]{0:T(128)}, u32[]{:S(2)}) copy-start(f32[128]{0:T(128)} %copy-done.81) | copy-start | bytes 1540
  255.8 17.4 %copy-start.53 = (bf16[2,16,16,512]{3,2,1,0:T(8,128)(2,1)S(1)}, bf16[2,16,16,512]{3,2,1,0:T(8,128)(2,1)}, u32[]{:S(2)}) copy-start(bf16[2,16,16,512]{3,2,1,0:T(8,128)(2,1)} %get-tuple-element.111) | copy-start | bytes 1572868
  256.9 16.7 %copy-start.52 = (bf16[2,16,16,512]{3,2,1,0:T(8,128)(2,1)S(1)}, bf16[2,16,16,512]{3,2,1,0:T(8,128)(2,1)}, u32[]{:S(2)}) copy-start(bf16[2,16,16,512]{3,2,1,0:T(8,128)(2,1)} %get-tuple-element.105) | copy-start | bytes 1572868
  288.5 2.0 copy-start.3
  288.5 2.0 copy-start.76
  288.6 2.0 copy-start.78
  288.6 2.3 copy-start.86
  288.6 44.1 %copy-start.87 = (f32[7,64]{1,0:T(8,128)S(1)}, f32[7,64]{1,0:T(8,128)}, u32[]{:S(2)}) copy-start(f32[7,64]{1,0:T(8,128)} %param.36) | copy-start | bytes 5380
  288.6 44.1 %copy-start.88 = (f32[7,64]{1,0:T(8,128)S(1)}, f32[7,64]{1,0:T(8,128)}, u32[]{:S(2)}) copy-start(f32[7,64]{1,0:T(8,128)} %param.35) | copy-start | bytes 5380
  288.6 44.7 %copy-start.70 = (f32[7,64,21]{1,2,0:T(8,128)S(1)}, f32[7,64,21]{1,2,0:T(8,128)}, u32[]{:S(2)}) copy-start(f32[7,64,21]{1,2,0:T(8,128)} %param.31) | copy-start | bytes 112900
  288.7 44.7 %copy-start.72 = (f32[7,64,21]{1,2,0:T(8,128)S(1)}, f32[7,64,21]{1,2,0:T(8,128)}, u32[]{:S(2)}) copy-start(f32[7,64,21]{1,2,0:T(8,128)} %param.33) | copy-start | bytes 112900
  288.7 44.7 %copy-start.73 = (f32[7,64,21]{1,2,0:T(8,128)S(1)}, f32[7,64,21]{1,2,0:T(8,128)}, u32[]{:S(2)}) copy-start(f32[7,64,21]{1,2,0:T(8,128)} %param.32) | copy-start | bytes 112900
  288.7 267.3 %copy-start = (f32[7,256,128]{2,1,0:T(8,128)S(1)}, f32[7,256,128]{2,1,0:T(8,128)}, u32[]{:S(2)}) copy-start(f32[7,256,128]{2,1,0:T(8,128)} %param.25) | copy-start | bytes 2752516
  288.7 267.3 %copy-start.93 = (s32[54]{0:T(128)S(1)}, s32[54]{0:T(128)}, u32[]{:S(2)}) copy-start(s32[54]{0:T(128)} %param.24) | copy-start | bytes 652
  564.8 2.2 copy-start.2
  564.8 2.2 copy-start.43
  564.8 2.2 copy-start.44
  564.8 2.7 copy-start.45
  (36 other events, 39.5 us)
Sparse Core Ops, SparseCore 0:
  10.8 69.0 all-gather.1
  132.5 30.8 all-reduce.9
  183.8 24.9 reduce-scatter.3
  216.6 24.7 reduce-scatter.5
  247.3 24.7 reduce-scatter.7
  288.7 267.2 all-reduce.11
where the time goes:
time: 586 us; the launch traced here: 577 us
  waiting for transfers between devices  335 us (57%)
  blocking collectives  116 us (20%)
  matrix products  58.8 us (10%)
  local copies, waits for them, and re-layouts  29.5 us (5%)
  other arithmetic  20.3 us (3%)
  between operations  16.6 us (3%)
    psum x1, waiting for transfers between devices, per_device(): summed_all = lax.psum(unit_grads, 'dp')  222 us
    reduce_scatter x3, waiting for transfers between devices, channel_sum(): lax.psum_scatter(partial_term, 'chan', scatter_dimension=3, tiled=True)  46.2 us
    psum x1, blocking collectives, per_device(): lax.psum((head_grad, join_grad, scale_grad, loss_local), 'dp')  41.8 us
    all_gather x1, waiting for transfers between devices, per_device(): lax.all_gather(conv_master.astype(jnp.bfloat16), 'dp', axis=0, tiled=True)  36.1 us
    psum x1, waiting for transfers between devices, per_device(): logits = lax.psum(partial_logits, 'chan')  30.9 us
    all_gather x4, blocking collectives, gather_channels(): return lax.all_gather(local_part, 'chan', axis=3, tiled=True)  29 us
    psum x1, blocking collectives, per_device(): lax.psum(jnp.sum(label_keep, axis=(0, 1, 2)), 'dp')  23.7 us
    dot_general x27, matrix products, conv_backward(): jnp.einsum('ihwc,ihwd->cd', window, grad_linear, preferred_element_type=j...  22.9 us
  transfers between devices with their start and end apart: 6, of which 6 were waited for; matrix products, arithmetic and copies ran while one was open for 6% of the time, Pallas kernels for 0%

commit v1 on v0

--- a/solution.py
+++ b/solution.py
@@ -165,7 +165,11 @@
             gathered, grad_linear, kernels[layer_index], layer_index > 0
         )
     unit_grads = jnp.stack(conv_grads).reshape(-1, C // 2, kernels.shape[3])
-    summed_all = lax.psum(unit_grads, "dp")
+    summed_all = unit_grads
+    for hop in (1, 2, 4):
+        summed_all = summed_all + lax.ppermute(
+            summed_all, "dp", [(dev, dev ^ hop) for dev in range(8)]
+        )
     slot_base = lax.axis_index("dp") * slot_count
     picking = ((slot_base + jnp.arange(slot_count))[:, None] == unit_slots[None, :]).astype(
         jnp.float32

time: 586 us -> 1010 us (1.72)
  blocking collectives: 116 us -> 405 us
  waiting for transfers between devices: 335 us -> 449 us
  other arithmetic: 20.3 us -> 41.5 us
    ppermute x0 -> x3, waiting for transfers between devices: none -> 304 us  [per_device(): lax.ppermute(summed_all, 'dp', [(dev, dev ^ hop) for dev in range(8)])]
    psum x1, blocking collectives: 41.8 us -> 328 us  [per_device(): lax.psum((head_grad, join_grad, scale_grad, loss_local), 'dp')]
    psum x1, waiting for transfers between devices: 222 us -> 32.7 us  [per_device(): lax.psum((head_grad, join_grad, scale_grad, loss_local), 'dp')]
    add x0 -> x3, other arithmetic: none -> 14.5 us  [per_device(): summed_all + lax.ppermute(summed_all, 'dp', [(dev, dev ^ hop) for dev in...]
  transfers between devices with their start and end apart: 6 -> 9, of which waited for: 6 -> 8; matrix products, arithmetic and copies ran while one was open for 6% -> 4% of each run, Pallas kernels for 0% -> 0%
where the time goes in v1:
time: 1010 us; the launch traced here: 1000 us
  waiting for transfers between devices  449 us (44%)
  blocking collectives  405 us (40%)
  matrix products  59.3 us (6%)
  other arithmetic  41.5 us (4%)
  local copies, waits for them, and re-layouts  27.4 us (3%)
  between operations  16.5 us (2%)
    psum x1, blocking collectives, per_device(): lax.psum((head_grad, join_grad, scale_grad, loss_local), 'dp')  328 us
    ppermute x3, waiting for transfers between devices, per_device(): lax.ppermute(summed_all, 'dp', [(dev, dev ^ hop) for dev in range(8)])  304 us
    reduce_scatter x3, waiting for transfers between devices, channel_sum(): lax.psum_scatter(partial_term, 'chan', scatter_dimension=3, tiled=True)  48.7 us
    all_gather x1, waiting for transfers between devices, per_device(): lax.all_gather(conv_master.astype(jnp.bfloat16), 'dp', axis=0, tiled=True)  33.9 us
    psum x1, waiting for transfers between devices, per_device(): lax.psum((head_grad, join_grad, scale_grad, loss_local), 'dp')  32.7 us
    psum x1, waiting for transfers between devices, per_device(): logits = lax.psum(partial_logits, 'chan')  29.6 us
    all_gather x4, blocking collectives, gather_channels(): return lax.all_gather(local_part, 'chan', axis=3, tiled=True)  29.4 us
    psum x1, blocking collectives, per_device(): lax.psum(jnp.sum(label_keep, axis=(0, 1, 2)), 'dp')  23.7 us
  transfers between devices with their start and end apart: 9, of which 8 were waited for; matrix products, arithmetic and copies ran while one was open for 4% of the time, Pallas kernels for 0%

profile of v1, /device:TPU:0, one launch (start us, length us, event | category | flops | bytes accessed | tf_op | source)
XLA Modules:
  0.0 1004.3 jit_solution(14706308550298641893)
XLA Ops:
  7.3 2.0 convert_element_type.77
  10.5 1.1 fusion.131
  11.5 23.7 %psum.56 = f32[7]{0:T(128)S(1)} all-reduce(f32[7]{0:T(128)S(1)} %get-tuple-element.73), channel_id=1, replica_groups=mesh['dp'=8,'chan'=4] {'dp'}, use_global_device_ids=true, to_apply=%region_1.2 | all-reduce | flops 7 | bytes 56 | tf_op jit(solution)/shard_map/psum | solution.py:112
  37.7 7.2 all_gather.15
  46.0 33.9 %all-gather.2.cloned.1.call-done = bf16[56,256,128]{2,1,0:T(8,128)(2,1)} async-done(((bf16[7,256,128]{2,1,0:T(8,128)(2,1)}), bf16[56,256,128]{2,1,0:T(8,128)(2,1)}) %all-gather.2.cloned.1.call-update) | async-done | bytes 3670032 | tf_op jit(solution)/shard_map/all_gather | solution.py:106
  79.9 4.9 gather_fusion
  84.8 2.4 broadcast_select_fusion
  91.1 7.2 all_gather.17
  101.9 7.3 all_gather.18
  112.8 7.7 all_gather.19
  120.5 2.1 multiply_reduce_fusion.2
  122.6 12.0 %psum.57 = f32[512,7]{0,1:T(8,128)} all-reduce(f32[512,7]{0,1:T(8,128)} %get-tuple-element.138), channel_id=1, replica_groups=mesh['dp'=8,'chan'=4] {'chan'}, use_global_device_ids=true, to_apply=%region_3.4 | all-reduce | flops 3584 | bytes 28672 | tf_op jit(solution)/shard_map/psum | solution.py:126
  135.9 1.9 convolution_bitcast_fusion.1
  137.9 1.4 broadcast_divide_fusion
  139.3 29.6 %all-reduce.9.cloned.1.call-done = f32[512,7,21]{0,2,1:T(8,128)} async-done(((f32[512,7,21]{0,2,1:T(8,128)}), f32[512,7,21]{0,2,1:T(8,128)}) %all-reduce.9.cloned.1.call-update) | async-done | bytes 301072 | tf_op jit(solution)/shard_map/psum | solution.py:133
  168.9 1.6 reduce_max.9
  170.5 1.7 fusion.61
  172.9 3.0 multiply_reduce_fusion
  175.8 11.8 %psum.60 = f32[512,7]{0,1:T(8,128)} all-reduce(f32[512,7]{0,1:T(8,128)} %get-tuple-element.53), channel_id=1, replica_groups=mesh['dp'=8,'chan'=4] {'chan'}, use_global_device_ids=true, to_apply=%region_11.12 | all-reduce | flops 3584 | bytes 28672 | tf_op jit(solution)/shard_map/psum | solution.py:151
  187.6 1.4 multiply_convert_fusion
  189.1 1.5 fusion.62
  190.7 2.3 pad_slice_fusion.16
  193.1 2.1 pad_slice_fusion
  195.2 2.3 pad_slice_fusion.8
  197.5 18.2 %reduce-scatter.4.cloned.1.call-done = f32[2,16,16,128]{3,2,1,0:T(8,128)} async-done(((f32[2,16,16,512]{3,2,1,0:T(8,128)}), f32[2,16,16,128]{3,2,1,0:T(8,128)}) %reduce-scatter.4.cloned.1.call-update) | async-done | bytes 262160 | tf_op jit(solution)/shard_map/reduce_scatter | solution.py:46
  215.7 1.1 select_convert_fusion.2
  220.2 1.3 convolution_add_fusion.8
  221.5 2.1 fusion.10
  223.6 2.1 fusion.9
  225.7 1.0 fusion.8
  226.8 1.0 fusion.7
  227.8 1.0 fusion.6
  228.9 1.1 fusion.5
  229.9 1.0 fusion.4
  231.0 1.1 fusion.3
  232.0 1.0 fusion.2
  233.1 13.3 %reduce-scatter.6.cloned.1.call-done = f32[2,16,16,128]{3,2,1,0:T(8,128)} async-done(((f32[2,16,16,512]{3,2,1,0:T(8,128)}), f32[2,16,16,128]{3,2,1,0:T(8,128)}) %reduce-scatter.6.cloned.1.call-update) | async-done | bytes 262160 | tf_op jit(solution)/shard_map/reduce_scatter | solution.py:46
  246.4 1.1 select_convert_fusion.1
  250.8 1.3 convolution_add_fusion
  252.4 1.4 fusion.19
  253.7 1.4 fusion.18
  259.9 17.2 %reduce-scatter.8.cloned.1.call-done = f32[2,16,16,128]{3,2,1,0:T(8,128)} async-done(((f32[2,16,16,512]{3,2,1,0:T(8,128)}), f32[2,16,16,128]{3,2,1,0:T(8,128)}) %reduce-scatter.8.cloned.1.call-update) | async-done | bytes 262160 | tf_op jit(solution)/shard_map/reduce_scatter | solution.py:46
  277.1 1.1 select_convert_fusion
  278.2 1.4 fusion.28
  284.6 2.3 pad_maximum_fusion
  286.9 1.5 collective-permute-start
  288.5 152.6 %collective-permute-done = f32[54,256,128]{2,1,0:T(8,128)} collective-permute-done((f32[54,256,128]{2,1,0:T(8,128)S(1)}, f32[54,256,128]{2,1,0:T(8,128)}, u32[]{:S(2)}, u32[]{:S(2)}) %collective-permute-start) | collective-permute-done | bytes 7077920 | tf_op jit(solution)/shard_map/ppermute | solution.py:170
  441.0 4.2 add.336
  445.2 1.6 collective-permute-start.1
  446.8 151.6 %collective-permute-done.1 = f32[54,256,128]{2,1,0:T(8,128)S(1)} collective-permute-done((f32[54,256,128]{2,1,0:T(8,128)S(1)}, f32[54,256,128]{2,1,0:T(8,128)S(1)}, u32[]{:S(2)}, u32[]{:S(2)}) %collective-permute-start.1) | collective-permute-done | bytes 7077920 | tf_op jit(solution)/shard_map/ppermute | solution.py:170
  598.4 4.0 add.337
  602.4 2.4 collective-permute-start.2
  606.1 2.4 fusion.135
  608.5 1.5 add_subtract_fusion
  610.8 1.3 multiply_reduce_fusion.3
  612.2 1.8 fusion.71
  614.0 327.7 %all-reduce.5 = (f32[1]{0:T(128)}, f32[7,64,21]{1,2,0:T(8,128)S(1)}, f32[7,64]{1,0:T(8,128)S(1)}) all-reduce(f32[1]{0:T(128)} %bitcast.90, f32[7,64,21]{1,2,0:T(8,128)} %fusion.71, f32[7,64]{1,0:T(8,128)S(1)} %copy-done.83), channel_id=1, replica_groups=mesh['dp'=8,'chan'=4] {'dp'}, use_global_device_ids=true, to_apply=%region_9.10 | all-reduce | flops 9857 | bytes 78856 | tf_op jit(solution)/shard_map/psum | solution.py:178
  943.1 32.7 %all-reduce.11.cloned.1.call-done = f32[7,64,512]{2,1,0:T(8,128)} async-done(((f32[7,64,512]{2,1,0:T(8,128)}), f32[7,64,512]{2,1,0:T(8,128)}) %all-reduce.11.cloned.1.call-update) | async-done | bytes 917520 | tf_op jit(solution)/shard_map/psum | solution.py:178
  975.8 3.5 multiply_subtract_fusion
  979.3 6.3 add.338
  985.7 8.3 copy_subtract_fusion
  994.0 1.1 copy.221
  995.1 1.1 copy.222
  996.2 1.1 copy.223
  (278 shorter events, 36.8 us)
Async XLA Ops:
  7.2 30.3 %copy-start.90 = (s32[54]{0:T(128)S(1)}, s32[54]{0:T(128)}, u32[]{:S(2)}) copy-start(s32[54]{0:T(128)} %param.24) | copy-start | bytes 652
  7.2 30.4 %copy-start.71 = (bf16[2,16,16,128]{3,2,1,0:T(8,128)(2,1)S(1)}, bf16[2,16,16,128]{3,2,1,0:T(8,128)(2,1)}, u32[]{:S(2)}) copy-start(bf16[2,16,16,128]{3,2,1,0:T(8,128)(2,1)} %param.19) | copy-start | bytes 393220
  7.2 38.3 %copy-start.86 = (f32[3,2,128]{2,1,0:T(2,128)S(1)}, f32[3,2,128]{2,1,0:T(2,128)}, u32[]{:S(2)}) copy-start(f32[3,2,128]{2,1,0:T(2,128)} %param.20) | copy-start | bytes 9220
  7.2 72.7 %all-gather.2.cloned.1.call-start = ((), (), s32[]{:S(2)}) async-start(), calls=%async_computation.3 | async-start | bytes 4128768 | tf_op jit(solution)/shard_map/all_gather | solution.py:106
  9.3 159.6 %all-reduce.9.cloned.1.call-start = ((), (), s32[]{:S(2)}) async-start(), calls=%async_computation.4 | async-start | bytes 688128 | tf_op jit(solution)/shard_map/psum | solution.py:133
  11.5 26.0 %copy-start.47 = (f32[2,16,16,7]{2,1,0,3:T(8,128)}, f32[2,16,16,7]{2,1,0,3:T(8,128)S(1)}, u32[]{:S(2)}) copy-start(f32[2,16,16,7]{2,1,0,3:T(8,128)S(1)} %get-tuple-element.74) | copy-start | bytes 43012
  87.3 11.0 %copy-start.24 = (bf16[2,256,128]{2,1,0:T(8,128)(2,1)}, bf16[2,256,128]{2,1,0:T(8,128)(2,1)S(1)}, u32[]{:S(2)}) copy-start(bf16[2,256,128]{2,1,0:T(8,128)(2,1)S(1)} %get-tuple-element.92) | copy-start | bytes 393220
  87.3 11.3 %copy-start.22 = (bf16[2,256,128]{2,1,0:T(8,128)(2,1)}, bf16[2,256,128]{2,1,0:T(8,128)(2,1)S(1)}, u32[]{:S(2)}) copy-start(bf16[2,256,128]{2,1,0:T(8,128)(2,1)S(1)} %get-tuple-element.91) | copy-start | bytes 393220
  87.3 11.6 %copy-start.20 = (bf16[2,256,128]{2,1,0:T(8,128)(2,1)}, bf16[2,256,128]{2,1,0:T(8,128)(2,1)S(1)}, u32[]{:S(2)}) copy-start(bf16[2,256,128]{2,1,0:T(8,128)(2,1)S(1)} %get-tuple-element.90) | copy-start | bytes 393220
  87.3 11.9 %copy-start.18 = (bf16[2,256,128]{2,1,0:T(8,128)(2,1)}, bf16[2,256,128]{2,1,0:T(8,128)(2,1)S(1)}, u32[]{:S(2)}) copy-start(bf16[2,256,128]{2,1,0:T(8,128)(2,1)S(1)} %get-tuple-element.89) | copy-start | bytes 393220
  87.4 12.2 %copy-start.16 = (bf16[2,256,128]{2,1,0:T(8,128)(2,1)}, bf16[2,256,128]{2,1,0:T(8,128)(2,1)S(1)}, u32[]{:S(2)}) copy-start(bf16[2,256,128]{2,1,0:T(8,128)(2,1)S(1)} %get-tuple-element.88) | copy-start | bytes 393220
  87.4 12.5 %copy-start.14 = (bf16[2,256,128]{2,1,0:T(8,128)(2,1)}, bf16[2,256,128]{2,1,0:T(8,128)(2,1)S(1)}, u32[]{:S(2)}) copy-start(bf16[2,256,128]{2,1,0:T(8,128)(2,1)S(1)} %get-tuple-element.87) | copy-start | bytes 393220
  87.4 12.8 %copy-start.12 = (bf16[2,256,128]{2,1,0:T(8,128)(2,1)}, bf16[2,256,128]{2,1,0:T(8,128)(2,1)S(1)}, u32[]{:S(2)}) copy-start(bf16[2,256,128]{2,1,0:T(8,128)(2,1)S(1)} %get-tuple-element.86) | copy-start | bytes 393220
  87.4 13.2 %copy-start.10 = (bf16[2,256,128]{2,1,0:T(8,128)(2,1)}, bf16[2,256,128]{2,1,0:T(8,128)(2,1)S(1)}, u32[]{:S(2)}) copy-start(bf16[2,256,128]{2,1,0:T(8,128)(2,1)S(1)} %get-tuple-element.85) | copy-start | bytes 393220
  87.4 21.8 %copy-start.42 = (bf16[2,256,128]{2,1,0:T(8,128)(2,1)}, bf16[2,256,128]{2,1,0:T(8,128)(2,1)S(1)}, u32[]{:S(2)}) copy-start(bf16[2,256,128]{2,1,0:T(8,128)(2,1)S(1)} %get-tuple-element.83) | copy-start | bytes 393220
  87.4 22.1 %copy-start.40 = (bf16[2,256,128]{2,1,0:T(8,128)(2,1)}, bf16[2,256,128]{2,1,0:T(8,128)(2,1)S(1)}, u32[]{:S(2)}) copy-start(bf16[2,256,128]{2,1,0:T(8,128)(2,1)S(1)} %get-tuple-element.82) | copy-start | bytes 393220
  87.4 22.4 %copy-start.38 = (bf16[2,256,128]{2,1,0:T(8,128)(2,1)}, bf16[2,256,128]{2,1,0:T(8,128)(2,1)S(1)}, u32[]{:S(2)}) copy-start(bf16[2,256,128]{2,1,0:T(8,128)(2,1)S(1)} %get-tuple-element.81) | copy-start | bytes 393220
  87.4 22.7 %copy-start.36 = (bf16[2,256,128]{2,1,0:T(8,128)(2,1)}, bf16[2,256,128]{2,1,0:T(8,128)(2,1)S(1)}, u32[]{:S(2)}) copy-start(bf16[2,256,128]{2,1,0:T(8,128)(2,1)S(1)} %get-tuple-element.80) | copy-start | bytes 393220
  87.4 23.0 %copy-start.34 = (bf16[2,256,128]{2,1,0:T(8,128)(2,1)}, bf16[2,256,128]{2,1,0:T(8,128)(2,1)S(1)}, u32[]{:S(2)}) copy-start(bf16[2,256,128]{2,1,0:T(8,128)(2,1)S(1)} %get-tuple-element.79) | copy-start | bytes 393220
  87.4 23.3 %copy-start.32 = (bf16[2,256,128]{2,1,0:T(8,128)(2,1)}, bf16[2,256,128]{2,1,0:T(8,128)(2,1)S(1)}, u32[]{:S(2)}) copy-start(bf16[2,256,128]{2,1,0:T(8,128)(2,1)S(1)} %get-tuple-element.78) | copy-start | bytes 393220
  87.5 23.6 %copy-start.30 = (bf16[2,256,128]{2,1,0:T(8,128)(2,1)}, bf16[2,256,128]{2,1,0:T(8,128)(2,1)S(1)}, u32[]{:S(2)}) copy-start(bf16[2,256,128]{2,1,0:T(8,128)(2,1)S(1)} %get-tuple-element.77) | copy-start | bytes 393220
  87.5 24.0 %copy-start.28 = (bf16[2,256,128]{2,1,0:T(8,128)(2,1)}, bf16[2,256,128]{2,1,0:T(8,128)(2,1)S(1)}, u32[]{:S(2)}) copy-start(bf16[2,256,128]{2,1,0:T(8,128)(2,1)S(1)} %get-tuple-element.76) | copy-start | bytes 393220
  87.5 24.3 %copy-start.26 = (bf16[2,256,128]{2,1,0:T(8,128)(2,1)}, bf16[2,256,128]{2,1,0:T(8,128)(2,1)S(1)}, u32[]{:S(2)}) copy-start(bf16[2,256,128]{2,1,0:T(8,128)(2,1)S(1)} %get-tuple-element.75) | copy-start | bytes 393220
  111.1 9.4 copy-start.3
  122.6 65.0 %copy-start = (f32[512,7,64]{0,2,1:T(8,128)}, f32[512,7,64]{0,2,1:T(8,128)S(1)}, u32[]{:S(2)}) copy-start(f32[512,7,64]{0,2,1:T(8,128)S(1)} %get-tuple-element.139) | copy-start | bytes 2752516
  137.9 77.8 %reduce-scatter.4.cloned.1.call-start = ((), (), s32[]{:S(2)}) async-start(), calls=%async_computation.5 | async-start | bytes 1310720 | tf_op jit(solution)/shard_map/reduce_scatter | solution.py:46
  190.6 55.8 %reduce-scatter.6.cloned.1.call-start = ((), (), s32[]{:S(2)}) async-start(), calls=%async_computation.6 | async-start | bytes 1310720 | tf_op jit(solution)/shard_map/reduce_scatter | solution.py:46
  195.2 20.4 %copy-start.82 = (f32[128]{0:T(128)S(1)}, f32[128]{0:T(128)}, u32[]{:S(2)}) copy-start(f32[128]{0:T(128)} %get-tuple-element.126) | copy-start | bytes 1540
  195.2 21.5 %copy-start.43 = (bf16[2,256,128]{2,1,0:T(8,128)(2,1)S(1)}, bf16[2,256,128]{2,1,0:T(8,128)(2,1)}, u32[]{:S(2)}) copy-start(bf16[2,256,128]{2,1,0:T(8,128)(2,1)} %copy-done.42) | copy-start | bytes 393220
  195.2 21.8 %copy-start.41 = (bf16[2,256,128]{2,1,0:T(8,128)(2,1)S(1)}, bf16[2,256,128]{2,1,0:T(8,128)(2,1)}, u32[]{:S(2)}) copy-start(bf16[2,256,128]{2,1,0:T(8,128)(2,1)} %copy-done.40) | copy-start | bytes 393220
  197.5 19.9 %copy-start.39 = (bf16[2,256,128]{2,1,0:T(8,128)(2,1)S(1)}, bf16[2,256,128]{2,1,0:T(8,128)(2,1)}, u32[]{:S(2)}) copy-start(bf16[2,256,128]{2,1,0:T(8,128)(2,1)} %copy-done.38) | copy-start | bytes 393220
  221.5 55.6 %reduce-scatter.8.cloned.1.call-start = ((), (), s32[]{:S(2)}) async-start(), calls=%async_computation.7 | async-start | bytes 1310720 | tf_op jit(solution)/shard_map/reduce_scatter | solution.py:46
  232.0 14.4 %copy-start.80 = (f32[128]{0:T(128)S(1)}, f32[128]{0:T(128)}, u32[]{:S(2)}) copy-start(f32[128]{0:T(128)} %get-tuple-element.128) | copy-start | bytes 1540
  232.0 15.4 %copy-start.25 = (bf16[2,256,128]{2,1,0:T(8,128)(2,1)S(1)}, bf16[2,256,128]{2,1,0:T(8,128)(2,1)}, u32[]{:S(2)}) copy-start(bf16[2,256,128]{2,1,0:T(8,128)(2,1)} %copy-done.24) | copy-start | bytes 393220
  232.0 15.8 %copy-start.23 = (bf16[2,256,128]{2,1,0:T(8,128)(2,1)S(1)}, bf16[2,256,128]{2,1,0:T(8,128)(2,1)}, u32[]{:S(2)}) copy-start(bf16[2,256,128]{2,1,0:T(8,128)(2,1)} %copy-done.22) | copy-start | bytes 393220
  233.1 15.0 %copy-start.21 = (bf16[2,256,128]{2,1,0:T(8,128)(2,1)S(1)}, bf16[2,256,128]{2,1,0:T(8,128)(2,1)}, u32[]{:S(2)}) copy-start(bf16[2,256,128]{2,1,0:T(8,128)(2,1)} %copy-done.20) | copy-start | bytes 393220
  252.1 723.7 %all-reduce.11.cloned.1.call-start = ((), (), s32[]{:S(2)}) async-start(), calls=%async_computation.8 | async-start | bytes 1835008 | tf_op jit(solution)/shard_map/psum | solution.py:178
  259.4 17.7 %copy-start.44 = (f32[2,16,16,128]{3,2,1,0:T(8,128)S(1)}, f32[2,16,16,128]{3,2,1,0:T(8,128)}, u32[]{:S(2)}) copy-start(f32[2,16,16,128]{3,2,1,0:T(8,128)} %get-tuple-element.133) | copy-start | bytes 786436
  259.4 17.7 %copy-start.78 = (f32[128]{0:T(128)S(1)}, f32[128]{0:T(128)}, u32[]{:S(2)}) copy-start(f32[128]{0:T(128)} %get-tuple-element.130) | copy-start | bytes 1540
  277.1 2.5 copy-start.56
  286.9 154.1 %collective-permute-start = (f32[54,256,128]{2,1,0:T(8,128)S(1)}, f32[54,256,128]{2,1,0:T(8,128)}, u32[]{:S(2)}, u32[]{:S(2)}) collective-permute-start(f32[54,256,128]{2,1,0:T(8,128)S(1)} %bitcast.449), channel_id=1, source_target_pairs={{0,4},{4,0},{8,12},{12,8},{16,20},{20,16},{24,28},{28,24},{1,5},{5... | collective-permute-start | bytes 21233672 | tf_op jit(solution)/shard_map/ppermute | solution.py:170
  445.2 160.9 %copy-start.6 = (bf16[512,7,64]{0,2,1:T(8,128)(2,1)S(1)}, bf16[512,7,64]{0,2,1:T(8,128)(2,1)}, u32[]{:S(2)}) copy-start(bf16[512,7,64]{0,2,1:T(8,128)(2,1)} %copy-done.5) | copy-start | bytes 1376260
  445.2 153.2 %collective-permute-start.1 = (f32[54,256,128]{2,1,0:T(8,128)S(1)}, f32[54,256,128]{2,1,0:T(8,128)S(1)}, u32[]{:S(2)}, u32[]{:S(2)}) collective-permute-start(f32[54,256,128]{2,1,0:T(8,128)S(1)} %add.336), channel_id=1, source_target_pairs={{0,8},{4,12},{8,0},{12,4},{16,24},{20,28},{24,16},{28,20},{1,9},{5... | collective-permute-start | bytes 21233672 | tf_op jit(solution)/shard_map/ppermute | solution.py:170
  602.4 6.1 copy-start.70
  602.4 6.2 copy-start.75
  602.4 8.5 copy-start.48
  602.4 9.8 copy-start.1
  602.4 9.8 copy-start.7
  602.4 9.8 copy-start.69
  602.4 376.9 %collective-permute-start.2 = (f32[54,256,128]{2,1,0:T(8,128)}, f32[54,256,128]{2,1,0:T(8,128)}, u32[]{:S(2)}, u32[]{:S(2)}) collective-permute-start(f32[54,256,128]{2,1,0:T(8,128)} %add.337), channel_id=1, source_target_pairs={{0,16},{4,20},{8,24},{12,28},{16,0},{20,4},{24,8},{28,12},{1,17},{... | collective-permute-start | bytes 21233672 | tf_op jit(solution)/shard_map/ppermute | solution.py:170
  608.5 5.5 copy-start.83
  608.5 333.3 %copy-start.76 = (f32[7,64]{1,0:T(8,128)S(1)}, f32[7,64]{1,0:T(8,128)}, u32[]{:S(2)}) copy-start(f32[7,64]{1,0:T(8,128)} %param.34) | copy-start | bytes 5380
  608.5 333.9 %copy-start.67 = (f32[7,64,21]{1,2,0:T(8,128)S(1)}, f32[7,64,21]{1,2,0:T(8,128)}, u32[]{:S(2)}) copy-start(f32[7,64,21]{1,2,0:T(8,128)} %param.31) | copy-start | bytes 112900
  608.5 333.9 %copy-start.72 = (f32[7,64,21]{1,2,0:T(8,128)S(1)}, f32[7,64,21]{1,2,0:T(8,128)}, u32[]{:S(2)}) copy-start(f32[7,64,21]{1,2,0:T(8,128)} %param.33) | copy-start | bytes 112900
  608.5 367.3 %copy-start.4 = (f32[7,64,512]{2,1,0:T(8,128)S(1)}, f32[7,64,512]{2,1,0:T(8,128)}, u32[]{:S(2)}) copy-start(f32[7,64,512]{2,1,0:T(8,128)} %param.28) | copy-start | bytes 2752516
  608.5 367.3 %copy-start.49 = (f32[7,64,512]{2,1,0:T(8,128)S(1)}, f32[7,64,512]{2,1,0:T(8,128)}, u32[]{:S(2)}) copy-start(f32[7,64,512]{2,1,0:T(8,128)} %param.30) | copy-start | bytes 2752516
  612.2 329.5 %copy-start.84 = (f32[7,64]{1,0:T(8,128)S(1)}, f32[7,64]{1,0:T(8,128)}, u32[]{:S(2)}) copy-start(f32[7,64]{1,0:T(8,128)} %param.36) | copy-start | bytes 5380
  612.2 329.6 %copy-start.85 = (f32[7,64]{1,0:T(8,128)S(1)}, f32[7,64]{1,0:T(8,128)}, u32[]{:S(2)}) copy-start(f32[7,64]{1,0:T(8,128)} %param.35) | copy-start | bytes 5380
  612.2 330.2 %copy-start.73 = (f32[7,64,21]{1,2,0:T(8,128)S(1)}, f32[7,64,21]{1,2,0:T(8,128)}, u32[]{:S(2)}) copy-start(f32[7,64,21]{1,2,0:T(8,128)} %param.32) | copy-start | bytes 112900
  979.3 6.4 copy-start.2
  979.3 6.4 copy-start.8
  979.3 6.4 copy-start.9
  979.3 6.4 copy-start.91
  979.3 6.4 copy-start.92
  (38 other events, 43.8 us)
Sparse Core Ops, SparseCore 0:
  10.8 69.0 all-gather.1
  138.0 30.8 all-reduce.8
  190.7 24.9 reduce-scatter.3
  221.6 24.7 reduce-scatter.5
  252.3 24.7 reduce-scatter.7
  608.6 367.1 all-reduce.10
